TPU v7x, 512 devices: a whole 4x4x16 slice. The times are simulated.
512 devices in a mesh: dom: 64 (over z, y), rep: 8 (over x, core).
Axes of the slice: x: 4, y: 4, z: 16, core: 2. Of those that a mesh axis runs over, the one named last changes fastest.
Arguments:
- feats: bfloat16 [65536, 128], P(('dom', 'rep')), may hold values from -6 to 6
- weight: bfloat16 [128, 128], replicated, may hold values from -0.5 to 0.5
- bias: float32 [128], replicated, may hold values from -3 to 3
- tiles: bfloat16 [512, 5, 28, 128, 128], P(('dom', 'rep')), may hold values from -0.0625 to 0.0625
- tile_cols: int32 [512, 5, 28], P(('dom', 'rep')), may hold values from 0 to 7
- tile_count: int32 [512, 5], P(('dom', 'rep')), may hold values from 2 to 28, as said below
- cotangent: bfloat16 [65536, 128], P(('dom', 'rep')), may hold values from -6 to 6
Outputs:
- hidden: bfloat16 [65536, 128], P(('dom', 'rep'))
- grad_weight: float32 [128, 128], replicated
- grad_bias: float32 [128], replicated
- grad_feats: bfloat16 [65536, 128], P(('dom', 'rep'))
Inputs may be any that keep to these rules, and one draw needn't show every extreme that they name: `tile_count`: every list has at least two live tiles; the nodes of some device have 28 live tiles in every list, and those of most devices far fewer.
All inputs are finite; a program needn't handle non-finite values.
Results may differ from a plain program's by a relative error of at most 0.0062.
Values may be sent and summed in bfloat16 or wider, within the bound.
A program may use at most 64 MiB of HBM per device.

v0:
```python
import jax
import jax.numpy as jnp
from jax import lax
from jax.sharding import PartitionSpec as P


def swapped(value, axis, bit):
    mask = 2**bit
    pairs = [(source, source ^ mask) for source in range(lax.axis_size(axis))]
    return lax.ppermute(value, axis, pairs)


def gelu_tanh(values):
    return jax.nn.gelu(values, approximate=True)


def add_slot(summed, panel, slot, tiles, tile_cols, live_mask):
    tgt_blocks, slot_count, max_tiles, block, unused = tiles.shape
    width = panel.shape[1]
    panel_blocks = panel.shape[0] // block
    source = panel.reshape(panel_blocks, block, width)
    columns = tile_cols[:, slot]
    slot_tiles = tiles[:, slot]
    fetched = source[columns]
    fetched = jnp.where(live_mask[:, slot][:, :, None, None], fetched, jnp.zeros((), jnp.bfloat16))
    return summed + jnp.einsum(
        "tmij,tmjh->tih", slot_tiles, fetched, preferred_element_type=jnp.float32
    )


def partial_panel(slot, tiles, tile_cols, live_mask, grad_rows_b, panel_blocks):
    tgt_blocks, slot_count, max_tiles, block, unused = tiles.shape
    width = grad_rows_b.shape[2]
    masked = jnp.where(
        live_mask[:, slot][:, :, None, None], tiles[:, slot], jnp.zeros((), jnp.bfloat16)
    )
    contrib = jnp.einsum("tmij,tih->tmjh", masked, grad_rows_b, preferred_element_type=jnp.float32)
    targets = tile_cols[:, slot].reshape(tgt_blocks * max_tiles)
    placed = jnp.zeros((panel_blocks, block, width), jnp.float32)
    placed = placed.at[targets].add(contrib.reshape(tgt_blocks * max_tiles, block, width))
    return placed.reshape(panel_blocks * block, width)


def body(feats, weight, bias, tiles, tile_cols, tile_count, cotangent):
    dom_size = lax.axis_size("dom")
    rep_size = lax.axis_size("rep")
    top_bit = dom_size.bit_length() - 1
    tgt_blocks, slot_count, max_tiles, block, unused = tiles.shape
    width = weight.shape[1]
    panel_blocks = rep_size * tgt_blocks
    live_mask = jnp.arange(max_tiles)[None, None, :] < tile_count[:, :, None]
    projected = jnp.dot(feats, weight, preferred_element_type=jnp.float32).astype(jnp.bfloat16)
    own_rows = lax.all_gather(projected, "rep", axis=0, tiled=True)
    summed = jnp.zeros((tgt_blocks, block, width), jnp.float32)
    summed = add_slot(summed, own_rows, 0, tiles, tile_cols, live_mask)
    for round_index in range(1, slot_count):
        bit_number = top_bit - round_index
        partner_rows = swapped(own_rows, "dom", bit_number)
        summed = add_slot(summed, partner_rows, round_index, tiles, tile_cols, live_mask)
    preact = summed.reshape(tgt_blocks * block, width) + bias
    hidden_f, pullback = jax.vjp(gelu_tanh, preact)
    hidden = hidden_f.astype(jnp.bfloat16)
    grad_pre = pullback(cotangent.astype(jnp.float32))[0]
    grad_rows_b = grad_pre.astype(jnp.bfloat16).reshape(tgt_blocks, block, width)
    grad_panel = partial_panel(0, tiles, tile_cols, live_mask, grad_rows_b, panel_blocks)
    for round_index in range(1, slot_count):
        outgoing = partial_panel(
            round_index, tiles, tile_cols, live_mask, grad_rows_b, panel_blocks
        )
        grad_panel = grad_panel + swapped(outgoing, "dom", top_bit - round_index)
    grad_proj = lax.psum_scatter(grad_panel, "rep", scatter_dimension=0, tiled=True).astype(
        jnp.bfloat16
    )
    weight_local = lax.dot_general(
        feats, grad_proj, (((0,), (0,)), ((), ())), preferred_element_type=jnp.float32
    )
    bias_local = jnp.sum(grad_pre, axis=0)
    grad_weight, grad_bias = lax.psum((weight_local, bias_local), ("dom", "rep"))
    grad_feats = lax.dot_general(
        grad_proj, weight, (((1,), (1,)), ((), ())), preferred_element_type=jnp.float32
    ).astype(jnp.bfloat16)
    return (hidden, grad_weight, grad_bias, grad_feats)


def solution(mesh):
    return jax.shard_map(
        body,
        mesh=mesh,
        in_specs=(
            P(("dom", "rep"), None),
            P(),
            P(),
            P(("dom", "rep"), None, None, None, None),
            P(("dom", "rep"), None, None),
            P(("dom", "rep"), None),
            P(("dom", "rep"), None),
        ),
        out_specs=(P(("dom", "rep"), None), P(), P(), P(("dom", "rep"), None)),
        check_vma=False,
    )
```

profile of v0, /device:TPU:1, one launch (start us, length us, event | category | flops | bytes accessed | tf_op | source)
XLA Modules:
  0.0 770.6 jit_solution(12770402989602264046)
XLA Ops:
  7.2 0.0 reduce-scatter.2.cloned.1.call-start
  7.2 0.7 copy-done
  7.9 0.9 convolution_convert_fusion.1
  8.8 19.5 %all_gather.3 = bf16[1024,128]{1,0:T(8,128)(2,1)S(1)} all-gather(bf16[128,128]{1,0:T(8,128)(2,1)S(1)} %convolution_convert_fusion.1), channel_id=1, replica_groups=mesh['dom'=64,'rep'=8] {'rep'}, dimensions={0}, use_global_device_ids=true | all-gather | bytes 294912 | tf_op jit(solution)/shard_map/all_gather | solution.py:53
  28.3 1.9 collective-permute-start.3
  30.2 1.9 collective-permute-start.2
  32.2 8.4 %collective-permute-start.1 = (bf16[1024,128]{1,0:T(8,128)(2,1)S(1)}, bf16[1024,128]{1,0:T(8,128)(2,1)S(1)}, u32[]{:S(2)}, u32[]{:S(2)}) collective-permute-start(bf16[1024,128]{1,0:T(8,128)(2,1)S(1)} %all_gather.3), channel_id=1, source_target_pairs={{0,128},{8,136},{16,144},{24,152},{32,160},{40,168},{48,176},{56,1... | collective-permute-start | bytes 786440 | tf_op jit(solution)/shard_map/ppermute | solution.py:10
  40.6 7.9 %collective-permute-start = (bf16[1024,128]{1,0:T(8,128)(2,1)S(1)}, bf16[1024,128]{1,0:T(8,128)(2,1)S(1)}, u32[]{:S(2)}, u32[]{:S(2)}) collective-permute-start(bf16[1024,128]{1,0:T(8,128)(2,1)S(1)} %all_gather.3), channel_id=1, source_target_pairs={{0,256},{8,264},{16,272},{24,280},{32,288},{40,296},{48,304},{56,3... | collective-permute-start | bytes 786440 | tf_op jit(solution)/shard_map/ppermute | solution.py:10
  48.5 0.7 fusion.81
  49.3 0.7 fusion.85
  50.0 0.7 iota_compare_fusion
  50.8 0.7 gather_fusion
  51.5 1.6 convolution_bitcast_fusion.4
  53.2 0.7 gather_fusion.4
  53.9 1.6 convolution_bitcast_fusion
  55.6 8.0 %collective-permute-done.2 = bf16[1024,128]{1,0:T(8,128)(2,1)S(1)} collective-permute-done((bf16[1024,128]{1,0:T(8,128)(2,1)S(1)}, bf16[1024,128]{1,0:T(8,128)(2,1)S(1)}, u32[]{:S(2)}, u32[]{:S(2)}) %collective-permute-start.2) | collective-permute-done | bytes 262176 | tf_op jit(solution)/shard_map/ppermute | solution.py:10
  63.6 0.7 gather_fusion.3
  64.3 1.6 convolution_bitcast_fusion.1
  66.0 19.9 %collective-permute-done.1 = bf16[1024,128]{1,0:T(8,128)(2,1)S(1)} collective-permute-done((bf16[1024,128]{1,0:T(8,128)(2,1)S(1)}, bf16[1024,128]{1,0:T(8,128)(2,1)S(1)}, u32[]{:S(2)}, u32[]{:S(2)}) %collective-permute-start.1) | collective-permute-done | bytes 262176 | tf_op jit(solution)/shard_map/ppermute | solution.py:10
  85.9 0.7 gather_fusion.2
  86.7 1.6 convolution_bitcast_fusion.2
  88.3 0.7 gather_fusion.1
  89.1 2.3 fusion.100
  91.4 3.2 fusion.12
  94.6 3.2 fusion.10
  97.8 2.0 fusion.8
  99.8 3.2 fusion.6
  103.0 4.6 scatter_fusion.1
  107.6 11.3 %collective-permute-start.4 = (f32[1024,128]{1,0:T(8,128)S(1)}, f32[1024,128]{1,0:T(8,128)}, u32[]{:S(2)}, u32[]{:S(2)}) collective-permute-start(f32[1024,128]{1,0:T(8,128)S(1)} %bitcast.141), channel_id=1, source_target_pairs={{0,256},{8,264},{16,272},{24,280},{32,288},{40,296},{48,304},{56,3... | collective-permute-start | bytes 1572872 | tf_op jit(solution)/shard_map/ppermute | solution.py:10
  118.9 4.6 scatter_fusion.2
  123.5 1.9 collective-permute-start.5
  125.5 2.6 scatter_fusion.3
  128.1 1.9 collective-permute-start.6
  130.1 4.6 scatter_fusion.4
  134.7 1.9 collective-permute-start.7
  136.6 3.2 fusion.14
  139.9 4.6 scatter_fusion
  144.5 8.2 %collective-permute-done.4 = f32[1024,128]{1,0:T(8,128)} collective-permute-done((f32[1024,128]{1,0:T(8,128)S(1)}, f32[1024,128]{1,0:T(8,128)}, u32[]{:S(2)}, u32[]{:S(2)}) %collective-permute-start.4) | collective-permute-done | bytes 524320 | tf_op jit(solution)/shard_map/ppermute | solution.py:10
  152.6 51.6 %collective-permute-done.5 = f32[1024,128]{1,0:T(8,128)} collective-permute-done((f32[1024,128]{1,0:T(8,128)S(1)}, f32[1024,128]{1,0:T(8,128)}, u32[]{:S(2)}, u32[]{:S(2)}) %collective-permute-start.5) | collective-permute-done | bytes 524320 | tf_op jit(solution)/shard_map/ppermute | solution.py:10
  204.2 2.3 fusion.53
  206.5 0.0 reduce-scatter.2.cloned.1.call-update
  206.5 0.0 all-reduce.2.cloned.1.call-start
  206.5 114.1 %psum.15 = f32[128]{0:T(128)} all-reduce(f32[128]{0:T(128)S(1)} %get-tuple-element.8), channel_id=1, replica_groups=mesh['dom'=64,'rep'=8] {'dom','rep'}, use_global_device_ids=true, to_apply=%region_8.9 | all-reduce | flops 128 | bytes 1024 | tf_op jit(solution)/shard_map/psum | solution.py:78
  320.7 1.7 convolution_bitcast_fusion.5
  322.3 0.0 all-reduce.2.cloned.1.call-update
  322.4 1.6 convolution_convert_fusion
  324.0 438.2 %all-reduce.2.cloned.1.call-done = f32[128,128]{0,1:T(8,128)} async-done(((f32[128,128]{0,1:T(8,128)}), f32[128,128]{0,1:T(8,128)}) %all-reduce.2.cloned.1.call-update) | async-done | bytes 65552 | tf_op jit(solution)/shard_map/psum | solution.py:78
  762.2 1.6 copy.16
  (23 shorter events, 0.3 us)
Async XLA Ops:
  7.2 0.8 copy-start
  7.2 313.5 %reduce-scatter.2.cloned.1.call-start = ((), (), s32[]{:S(2)}) async-start(), calls=%async_computation.1 | async-start | bytes 589824 | tf_op jit(solution)/shard_map/reduce_scatter | solution.py:71
  28.3 24.9 %collective-permute-start.3 = (bf16[1024,128]{1,0:T(8,128)(2,1)S(1)}, bf16[1024,128]{1,0:T(8,128)(2,1)S(1)}, u32[]{:S(2)}, u32[]{:S(2)}) collective-permute-start(bf16[1024,128]{1,0:T(8,128)(2,1)S(1)} %all_gather.3), channel_id=1, source_target_pairs={{0,32},{8,40},{16,48},{24,56},{32,0},{40,8},{48,16},{56,24},{64,96... | collective-permute-start | bytes 786440 | tf_op jit(solution)/shard_map/ppermute | solution.py:10
  30.2 33.4 %collective-permute-start.2 = (bf16[1024,128]{1,0:T(8,128)(2,1)S(1)}, bf16[1024,128]{1,0:T(8,128)(2,1)S(1)}, u32[]{:S(2)}, u32[]{:S(2)}) collective-permute-start(bf16[1024,128]{1,0:T(8,128)(2,1)S(1)} %all_gather.3), channel_id=1, source_target_pairs={{0,64},{8,72},{16,80},{24,88},{32,96},{40,104},{48,112},{56,120},{... | collective-permute-start | bytes 786440 | tf_op jit(solution)/shard_map/ppermute | solution.py:10
  32.2 53.7 %collective-permute-start.1 = (bf16[1024,128]{1,0:T(8,128)(2,1)S(1)}, bf16[1024,128]{1,0:T(8,128)(2,1)S(1)}, u32[]{:S(2)}, u32[]{:S(2)}) collective-permute-start(bf16[1024,128]{1,0:T(8,128)(2,1)S(1)} %all_gather.3), channel_id=1, source_target_pairs={{0,128},{8,136},{16,144},{24,152},{32,160},{40,168},{48,176},{56,1... | collective-permute-start | bytes 786440 | tf_op jit(solution)/shard_map/ppermute | solution.py:10
  40.6 47.7 %collective-permute-start = (bf16[1024,128]{1,0:T(8,128)(2,1)S(1)}, bf16[1024,128]{1,0:T(8,128)(2,1)S(1)}, u32[]{:S(2)}, u32[]{:S(2)}) collective-permute-start(bf16[1024,128]{1,0:T(8,128)(2,1)S(1)} %all_gather.3), channel_id=1, source_target_pairs={{0,256},{8,264},{16,272},{24,280},{32,288},{40,296},{48,304},{56,3... | collective-permute-start | bytes 786440 | tf_op jit(solution)/shard_map/ppermute | solution.py:10
  86.6 2.4 copy-start.2
  86.6 2.4 copy-start.3
  107.6 45.0 %collective-permute-start.4 = (f32[1024,128]{1,0:T(8,128)S(1)}, f32[1024,128]{1,0:T(8,128)}, u32[]{:S(2)}, u32[]{:S(2)}) collective-permute-start(f32[1024,128]{1,0:T(8,128)S(1)} %bitcast.141), channel_id=1, source_target_pairs={{0,256},{8,264},{16,272},{24,280},{32,288},{40,296},{48,304},{56,3... | collective-permute-start | bytes 1572872 | tf_op jit(solution)/shard_map/ppermute | solution.py:10
  123.5 80.7 %collective-permute-start.5 = (f32[1024,128]{1,0:T(8,128)S(1)}, f32[1024,128]{1,0:T(8,128)}, u32[]{:S(2)}, u32[]{:S(2)}) collective-permute-start(f32[1024,128]{1,0:T(8,128)S(1)} %bitcast.142), channel_id=1, source_target_pairs={{0,128},{8,136},{16,144},{24,152},{32,160},{40,168},{48,176},{56,1... | collective-permute-start | bytes 1572872 | tf_op jit(solution)/shard_map/ppermute | solution.py:10
  128.1 76.1 %collective-permute-start.6 = (f32[1024,128]{1,0:T(8,128)S(1)}, f32[1024,128]{1,0:T(8,128)S(1)}, u32[]{:S(2)}, u32[]{:S(2)}) collective-permute-start(f32[1024,128]{1,0:T(8,128)S(1)} %bitcast.143), channel_id=1, source_target_pairs={{0,64},{8,72},{16,80},{24,88},{32,96},{40,104},{48,112},{56,120},{... | collective-permute-start | bytes 1572872 | tf_op jit(solution)/shard_map/ppermute | solution.py:10
  134.7 69.5 %collective-permute-start.7 = (f32[1024,128]{1,0:T(8,128)S(1)}, f32[1024,128]{1,0:T(8,128)}, u32[]{:S(2)}, u32[]{:S(2)}) collective-permute-start(f32[1024,128]{1,0:T(8,128)S(1)} %bitcast.144), channel_id=1, source_target_pairs={{0,32},{8,40},{16,48},{24,56},{32,0},{40,8},{48,16},{56,24},{64,96... | collective-permute-start | bytes 1572872 | tf_op jit(solution)/shard_map/ppermute | solution.py:10
  144.4 177.9 %copy-start.1 = (bf16[128,128]{1,0:T(8,128)(2,1)S(1)}, bf16[128,128]{1,0:T(8,128)(2,1)}, u32[]{:S(2)}) copy-start(bf16[128,128]{1,0:T(8,128)(2,1)} %param.8) | copy-start | bytes 98308
  206.5 555.7 %all-reduce.2.cloned.1.call-start = ((), (), s32[]{:S(2)}) async-start(), calls=%async_computation.2 | async-start | bytes 131072 | tf_op jit(solution)/shard_map/psum | solution.py:78
Sparse Core Ops, SparseCore 0:
  206.6 44.0 reduce-scatter.1
  322.5 439.6 all-reduce.1
where the time goes:
time: 772 us; the launch traced here: 771 us
  waiting for transfers between devices  526 us (68%)
  blocking collectives  134 us (17%)
  starting transfers between devices  37.3 us (5%)
  matrix products  27.8 us (4%)
  other arithmetic  25.4 us (3%)
  between operations  14.3 us (2%)
    psum x1, waiting for transfers between devices, body(): lax.psum((weight_local, bias_local), ('dom', 'rep'))  438 us
    psum x1, blocking collectives, body(): lax.psum((weight_local, bias_local), ('dom', 'rep'))  114 us
    ppermute x8, waiting for transfers between devices, swapped(): return lax.ppermute(value, axis, pairs)  87.7 us
    ppermute x8, starting transfers between devices, swapped(): return lax.ppermute(value, axis, pairs)  37.2 us
    scatter-add x5, other arithmetic, partial_panel(): placed.at[targets]  20.9 us
    all_gather x1, blocking collectives, body(): own_rows = lax.all_gather(projected, 'rep', axis=0, tiled=True)  19.5 us
  transfers between devices with their start and end apart: 10, of which 5 were waited for; matrix products, arithmetic and copies ran while one was open for 4% of the time, Pallas kernels for 0%

commit v1 on v0

--- a/solution.py
+++ b/solution.py
@@ -1,7 +1,15 @@
+import functools
 import jax
 import jax.numpy as jnp
 from jax import lax
 from jax.sharding import PartitionSpec as P
+
+
+def zones_supply_all(sample, axis_key, comm_axis):
+    return lax.psum(lax.psum(sample, axis_name=axis_key), axis_name=comm_axis)
+
+
+take_the_heaps = functools.partial(zones_supply_all, axis_key="dom", comm_axis="rep")
 
 
 def swapped(value, axis, bit):
@@ -75,7 +83,7 @@
         feats, grad_proj, (((0,), (0,)), ((), ())), preferred_element_type=jnp.float32
     )
     bias_local = jnp.sum(grad_pre, axis=0)
-    grad_weight, grad_bias = lax.psum((weight_local, bias_local), ("dom", "rep"))
+    grad_weight, grad_bias = take_the_heaps((weight_local, bias_local))
     grad_feats = lax.dot_general(
         grad_proj, weight, (((1,), (1,)), ((), ())), preferred_element_type=jnp.float32
     ).astype(jnp.bfloat16)

time: 772 us -> 597 us (0.77)
  waiting for transfers between devices: 526 us -> 307 us
  blocking collectives: 134 us -> 178 us
    psum x1 -> x2, waiting for transfers between devices: 438 us -> 175 us  [zones_supply_all(): return lax.psum(lax.psum(sample, axis_name=axis_key), axis_name=comm_axis)]
    psum x1 -> x2, blocking collectives: 114 us -> 159 us  [zones_supply_all(): return lax.psum(lax.psum(sample, axis_name=axis_key), axis_name=comm_axis)]
    reduce_scatter x1, waiting for transfers between devices: 0.01 us -> 44.2 us  [body(): lax.psum_scatter(grad_panel, 'rep', scatter_dimension=0, tiled=True)]
  transfers between devices with their start and end apart: 10 -> 11, of which waited for: 5 -> 7; matrix products, arithmetic and copies ran while one was open for 4% -> 6% of each run, Pallas kernels for 0% -> 0%
where the time goes in v1:
time: 597 us; the launch traced here: 595 us
  waiting for transfers between devices  307 us (51%)
  blocking collectives  178 us (30%)
  starting transfers between devices  37.4 us (6%)
  matrix products  27.8 us (5%)
  other arithmetic  25.4 us (4%)
  between operations  14 us (2%)
  local copies, waits for them, and re-layouts  6.1 us (1%)
    psum x2, waiting for transfers between devices, zones_supply_all(): return lax.psum(lax.psum(sample, axis_name=axis_key), axis_name=comm_axis)  175 us
    psum x2, blocking collectives, zones_supply_all(): return lax.psum(lax.psum(sample, axis_name=axis_key), axis_name=comm_axis)  159 us
    ppermute x8, waiting for transfers between devices, swapped(): return lax.ppermute(value, axis, pairs)  87.7 us
    reduce_scatter x1, waiting for transfers between devices, body(): lax.psum_scatter(grad_panel, 'rep', scatter_dimension=0, tiled=True)  44.2 us
    ppermute x8, starting transfers between devices, swapped(): return lax.ppermute(value, axis, pairs)  37.2 us
    scatter-add x5, other arithmetic, partial_panel(): placed.at[targets]  20.9 us
    all_gather x1, blocking collectives, body(): own_rows = lax.all_gather(projected, 'rep', axis=0, tiled=True)  19.5 us
    dot_general x5, matrix products, partial_panel(): jnp.einsum('tmij,tih->tmjh', masked, grad_rows_b, preferred_element_type=...  14.8 us
  transfers between devices with their start and end apart: 11, of which 7 were waited for; matrix products, arithmetic and copies ran while one was open for 6% of the time, Pallas kernels for 0%

profile of v1, /device:TPU:1, one launch (start us, length us, event | category | flops | bytes accessed | tf_op | source)
XLA Modules:
  0.0 595.4 jit_solution(16742236536779313913)
XLA Ops:
  7.2 0.7 copy-done
  7.9 0.9 convolution_convert_fusion.1
  8.8 19.5 %all_gather.3 = bf16[1024,128]{1,0:T(8,128)(2,1)S(1)} all-gather(bf16[128,128]{1,0:T(8,128)(2,1)S(1)} %convolution_convert_fusion.1), channel_id=1, replica_groups=mesh['dom'=64,'rep'=8] {'rep'}, dimensions={0}, use_global_device_ids=true | all-gather | bytes 294912 | tf_op jit(solution)/shard_map/all_gather | solution.py:61
  28.3 1.9 collective-permute-start.3
  30.2 1.9 collective-permute-start.2
  32.2 8.4 %collective-permute-start.1 = (bf16[1024,128]{1,0:T(8,128)(2,1)S(1)}, bf16[1024,128]{1,0:T(8,128)(2,1)S(1)}, u32[]{:S(2)}, u32[]{:S(2)}) collective-permute-start(bf16[1024,128]{1,0:T(8,128)(2,1)S(1)} %all_gather.3), channel_id=1, source_target_pairs={{0,128},{8,136},{16,144},{24,152},{32,160},{40,168},{48,176},{56,1... | collective-permute-start | bytes 786440 | tf_op jit(solution)/shard_map/ppermute | solution.py:18
  40.6 7.9 %collective-permute-start = (bf16[1024,128]{1,0:T(8,128)(2,1)S(1)}, bf16[1024,128]{1,0:T(8,128)(2,1)S(1)}, u32[]{:S(2)}, u32[]{:S(2)}) collective-permute-start(bf16[1024,128]{1,0:T(8,128)(2,1)S(1)} %all_gather.3), channel_id=1, source_target_pairs={{0,256},{8,264},{16,272},{24,280},{32,288},{40,296},{48,304},{56,3... | collective-permute-start | bytes 786440 | tf_op jit(solution)/shard_map/ppermute | solution.py:18
  48.5 0.7 fusion.81
  49.3 0.7 fusion.85
  50.0 0.7 iota_compare_fusion
  50.8 0.7 gather_fusion
  51.5 1.6 convolution_bitcast_fusion.4
  53.2 0.7 gather_fusion.4
  53.9 1.6 convolution_bitcast_fusion
  55.6 8.0 %collective-permute-done.2 = bf16[1024,128]{1,0:T(8,128)(2,1)S(1)} collective-permute-done((bf16[1024,128]{1,0:T(8,128)(2,1)S(1)}, bf16[1024,128]{1,0:T(8,128)(2,1)S(1)}, u32[]{:S(2)}, u32[]{:S(2)}) %collective-permute-start.2) | collective-permute-done | bytes 262176 | tf_op jit(solution)/shard_map/ppermute | solution.py:18
  63.6 0.7 gather_fusion.3
  64.3 1.6 convolution_bitcast_fusion.1
  66.0 19.9 %collective-permute-done.1 = bf16[1024,128]{1,0:T(8,128)(2,1)S(1)} collective-permute-done((bf16[1024,128]{1,0:T(8,128)(2,1)S(1)}, bf16[1024,128]{1,0:T(8,128)(2,1)S(1)}, u32[]{:S(2)}, u32[]{:S(2)}) %collective-permute-start.1) | collective-permute-done | bytes 262176 | tf_op jit(solution)/shard_map/ppermute | solution.py:18
  85.9 0.7 gather_fusion.2
  86.7 1.6 convolution_bitcast_fusion.2
  88.3 0.7 gather_fusion.1
  89.1 2.3 fusion.100
  91.4 3.2 fusion.12
  94.6 3.2 fusion.10
  97.8 2.0 fusion.8
  99.8 3.2 fusion.6
  103.0 4.6 scatter_fusion.1
  107.6 11.3 %collective-permute-start.4 = (f32[1024,128]{1,0:T(8,128)S(1)}, f32[1024,128]{1,0:T(8,128)}, u32[]{:S(2)}, u32[]{:S(2)}) collective-permute-start(f32[1024,128]{1,0:T(8,128)S(1)} %bitcast.141), channel_id=1, source_target_pairs={{0,256},{8,264},{16,272},{24,280},{32,288},{40,296},{48,304},{56,3... | collective-permute-start | bytes 1572872 | tf_op jit(solution)/shard_map/ppermute | solution.py:18
  118.9 4.6 scatter_fusion.2
  123.5 1.9 collective-permute-start.5
  125.5 2.6 scatter_fusion.3
  128.1 1.9 collective-permute-start.6
  130.1 4.6 scatter_fusion.4
  134.7 1.9 collective-permute-start.7
  136.6 3.2 fusion.14
  139.9 4.6 scatter_fusion
  144.5 8.2 %collective-permute-done.4 = f32[1024,128]{1,0:T(8,128)} collective-permute-done((f32[1024,128]{1,0:T(8,128)S(1)}, f32[1024,128]{1,0:T(8,128)}, u32[]{:S(2)}, u32[]{:S(2)}) %collective-permute-start.4) | collective-permute-done | bytes 524320 | tf_op jit(solution)/shard_map/ppermute | solution.py:18
  152.6 51.6 %collective-permute-done.5 = f32[1024,128]{1,0:T(8,128)} collective-permute-done((f32[1024,128]{1,0:T(8,128)S(1)}, f32[1024,128]{1,0:T(8,128)}, u32[]{:S(2)}, u32[]{:S(2)}) %collective-permute-start.5) | collective-permute-done | bytes 524320 | tf_op jit(solution)/shard_map/ppermute | solution.py:18
  204.2 2.3 fusion.53
  206.5 0.0 all-reduce.3.cloned.1.call-start
  206.5 44.2 %reduce-scatter.2.cloned.1.call-done = f32[128,128]{1,0:T(8,128)} async-done(((f32[1024,128]{1,0:T(8,128)}), f32[128,128]{1,0:T(8,128)}) %reduce-scatter.2.cloned.1.call-update) | async-done | bytes 65552 | tf_op jit(solution)/shard_map/reduce_scatter | solution.py:79
  250.7 1.7 convolution_bitcast_fusion.5
  252.4 116.1 %psum.30 = f32[128]{0:T(128)S(1)} all-reduce(f32[128]{0:T(128)S(1)} %get-tuple-element.8), channel_id=1, replica_groups=mesh['dom'=64,'rep'=8] {'dom'}, use_global_device_ids=true, to_apply=%region_9.10 | all-reduce | flops 128 | bytes 1024 | tf_op jit(solution)/shard_map/psum | solution.py:9
  368.5 42.5 %psum.31 = f32[128]{0:T(128)} all-reduce(f32[128]{0:T(128)S(1)} %psum.30), channel_id=1, replica_groups=mesh['dom'=64,'rep'=8] {'rep'}, use_global_device_ids=true, to_apply=%region_10.11 | all-reduce | flops 128 | bytes 1024 | tf_op jit(solution)/shard_map/psum | solution.py:9
  411.1 95.5 %all-reduce.3.cloned.1.call-done = f32[128,128]{0,1:T(8,128)} async-done(((f32[128,128]{0,1:T(8,128)}), f32[128,128]{0,1:T(8,128)}) %all-reduce.3.cloned.1.call-update) | async-done | bytes 65552 | tf_op jit(solution)/shard_map/psum | solution.py:9
  506.6 1.6 convolution_convert_fusion
  508.2 79.1 %all-reduce.5.cloned.1.call-done = f32[128,128]{0,1:T(8,128)} async-done(((f32[128,128]{0,1:T(8,128)}), f32[128,128]{0,1:T(8,128)}) %all-reduce.5.cloned.1.call-update) | async-done | bytes 65552 | tf_op jit(solution)/shard_map/psum | solution.py:9
  587.3 1.6 copy.16
  (27 shorter events, 0.4 us)
Async XLA Ops:
  7.2 0.8 copy-start
  7.2 243.5 %reduce-scatter.2.cloned.1.call-start = ((), (), s32[]{:S(2)}) async-start(), calls=%async_computation.1 | async-start | bytes 589824 | tf_op jit(solution)/shard_map/reduce_scatter | solution.py:79
  28.3 24.9 %collective-permute-start.3 = (bf16[1024,128]{1,0:T(8,128)(2,1)S(1)}, bf16[1024,128]{1,0:T(8,128)(2,1)S(1)}, u32[]{:S(2)}, u32[]{:S(2)}) collective-permute-start(bf16[1024,128]{1,0:T(8,128)(2,1)S(1)} %all_gather.3), channel_id=1, source_target_pairs={{0,32},{8,40},{16,48},{24,56},{32,0},{40,8},{48,16},{56,24},{64,96... | collective-permute-start | bytes 786440 | tf_op jit(solution)/shard_map/ppermute | solution.py:18
  30.2 33.4 %collective-permute-start.2 = (bf16[1024,128]{1,0:T(8,128)(2,1)S(1)}, bf16[1024,128]{1,0:T(8,128)(2,1)S(1)}, u32[]{:S(2)}, u32[]{:S(2)}) collective-permute-start(bf16[1024,128]{1,0:T(8,128)(2,1)S(1)} %all_gather.3), channel_id=1, source_target_pairs={{0,64},{8,72},{16,80},{24,88},{32,96},{40,104},{48,112},{56,120},{... | collective-permute-start | bytes 786440 | tf_op jit(solution)/shard_map/ppermute | solution.py:18
  32.2 53.7 %collective-permute-start.1 = (bf16[1024,128]{1,0:T(8,128)(2,1)S(1)}, bf16[1024,128]{1,0:T(8,128)(2,1)S(1)}, u32[]{:S(2)}, u32[]{:S(2)}) collective-permute-start(bf16[1024,128]{1,0:T(8,128)(2,1)S(1)} %all_gather.3), channel_id=1, source_target_pairs={{0,128},{8,136},{16,144},{24,152},{32,160},{40,168},{48,176},{56,1... | collective-permute-start | bytes 786440 | tf_op jit(solution)/shard_map/ppermute | solution.py:18
  40.6 47.7 %collective-permute-start = (bf16[1024,128]{1,0:T(8,128)(2,1)S(1)}, bf16[1024,128]{1,0:T(8,128)(2,1)S(1)}, u32[]{:S(2)}, u32[]{:S(2)}) collective-permute-start(bf16[1024,128]{1,0:T(8,128)(2,1)S(1)} %all_gather.3), channel_id=1, source_target_pairs={{0,256},{8,264},{16,272},{24,280},{32,288},{40,296},{48,304},{56,3... | collective-permute-start | bytes 786440 | tf_op jit(solution)/shard_map/ppermute | solution.py:18
  86.6 2.4 copy-start.2
  86.6 2.4 copy-start.3
  107.6 45.0 %collective-permute-start.4 = (f32[1024,128]{1,0:T(8,128)S(1)}, f32[1024,128]{1,0:T(8,128)}, u32[]{:S(2)}, u32[]{:S(2)}) collective-permute-start(f32[1024,128]{1,0:T(8,128)S(1)} %bitcast.141), channel_id=1, source_target_pairs={{0,256},{8,264},{16,272},{24,280},{32,288},{40,296},{48,304},{56,3... | collective-permute-start | bytes 1572872 | tf_op jit(solution)/shard_map/ppermute | solution.py:18
  123.5 80.7 %collective-permute-start.5 = (f32[1024,128]{1,0:T(8,128)S(1)}, f32[1024,128]{1,0:T(8,128)}, u32[]{:S(2)}, u32[]{:S(2)}) collective-permute-start(f32[1024,128]{1,0:T(8,128)S(1)} %bitcast.142), channel_id=1, source_target_pairs={{0,128},{8,136},{16,144},{24,152},{32,160},{40,168},{48,176},{56,1... | collective-permute-start | bytes 1572872 | tf_op jit(solution)/shard_map/ppermute | solution.py:18
  128.1 76.1 %collective-permute-start.6 = (f32[1024,128]{1,0:T(8,128)S(1)}, f32[1024,128]{1,0:T(8,128)S(1)}, u32[]{:S(2)}, u32[]{:S(2)}) collective-permute-start(f32[1024,128]{1,0:T(8,128)S(1)} %bitcast.143), channel_id=1, source_target_pairs={{0,64},{8,72},{16,80},{24,88},{32,96},{40,104},{48,112},{56,120},{... | collective-permute-start | bytes 1572872 | tf_op jit(solution)/shard_map/ppermute | solution.py:18
  134.7 69.5 %collective-permute-start.7 = (f32[1024,128]{1,0:T(8,128)S(1)}, f32[1024,128]{1,0:T(8,128)}, u32[]{:S(2)}, u32[]{:S(2)}) collective-permute-start(f32[1024,128]{1,0:T(8,128)S(1)} %bitcast.144), channel_id=1, source_target_pairs={{0,32},{8,40},{16,48},{24,56},{32,0},{40,8},{48,16},{56,24},{64,96... | collective-permute-start | bytes 1572872 | tf_op jit(solution)/shard_map/ppermute | solution.py:18
  144.4 362.1 %copy-start.1 = (bf16[128,128]{1,0:T(8,128)(2,1)S(1)}, bf16[128,128]{1,0:T(8,128)(2,1)}, u32[]{:S(2)}) copy-start(bf16[128,128]{1,0:T(8,128)(2,1)} %param.8) | copy-start | bytes 98308
  206.5 300.0 %all-reduce.3.cloned.1.call-start = ((), (), s32[]{:S(2)}) async-start(), calls=%async_computation.2 | async-start | bytes 131072 | tf_op jit(solution)/shard_map/psum | solution.py:9
  252.4 334.9 %all-reduce.5.cloned.1.call-start = ((), (), s32[]{:S(2)}) async-start(), calls=%async_computation.3 | async-start | bytes 131072 | tf_op jit(solution)/shard_map/psum | solution.py:9
Sparse Core Ops, SparseCore 0:
  206.6 44.0 reduce-scatter.1
  254.7 251.7 all-reduce.2
  508.9 78.4 all-reduce.4
